TPU v7x, 32 devices: a whole 2x2x4 slice. The times are simulated.
32 devices in a mesh: ty: 4 (over y, x), tx: 4 (over z), slide: 2 (over core).
Axes of the slice: x: 2, y: 2, z: 4, core: 2. Of those that a mesh axis runs over, the one named last changes fastest.
Arguments:
- tokens: bfloat16 [8, 4, 192, 768], P(('slide', 'ty'), 'tx'), parts along dimension 0, may hold values from -6 to 6
- summary: bfloat16 [512, 768], P(('slide', 'ty', 'tx')), parts along dimension 0, may hold values from -6 to 6
- counts: int32 [8, 4], P('slide'), parts along dimension 0, may hold values from 1 to 192, as said below
- tile_pattern: int32 [8, 4, 9], P('slide'), parts along dimension 0, may hold values from 0 to 1, as said below
- summary_pattern: int32 [8, 4, 2], P(('slide', 'ty'), 'tx'), parts along dimension 0, may hold values 0 or 1
- norm_gain: float32 [768], replicated, may hold values from 0.1 to 1.9
- projections: bfloat16 [4, 768, 768], replicated, may hold values from -4 to 4
- cotangent: bfloat16 [8, 4, 192, 768], P(('slide', 'ty'), 'tx'), parts along dimension 0, may hold values from -6 to 6
Outputs:
- updated: bfloat16 [8, 4, 192, 768], P(('slide', 'ty'), 'tx'), parts along dimension 0
- grad_tokens: bfloat16 [8, 4, 192, 768], P(('slide', 'ty'), 'tx'), parts along dimension 0
- grad_summary: bfloat16 [512, 768], P(('slide', 'ty', 'tx')), parts along dimension 0
- grad_proj: float32 [8, 768, 768], P('slide'), parts along dimension 0
- grad_gain: float32 [1536], P('slide'), parts along dimension 0
There are 2 independent parts, one for each index of `slide`. A program takes and returns all parts, laid end to end along the dimension named above; an argument that names none is the same for every part. Nothing has to cross between parts.
Inputs may be any that keep to these rules, and one draw needn't show every extreme that they name: `counts`: some tile holds exactly 192 tokens and some tile exactly 1 in every draw. `tile_pattern`: entry 4, the tile itself, is always 1.
All inputs are finite; a program needn't handle non-finite values. No bound on the sum of `summary_pattern` on one device may be relied on, other than what follows from the above.
Results may differ from a plain program's by a relative error of at most 0.011.
Values may be sent and summed in bfloat16 or wider, within the bound.
No kernel may reach another device: no remote copies, remote signals or barrier semaphores. Data moves between devices by JAX's collectives and lax.ppermute only.
A program may use at most 128 MiB of HBM per device.

v0:
```python
import math
import jax
import jax.numpy as jnp
from jax import lax
from jax.sharding import PartitionSpec as P

HEADS = 12
SBLK = 128
epsilon = 1e-05


def with_halo(cells, sides, width):
    for axis, dim in sides:
        count = lax.axis_size(axis)
        ends = count - 1
        head = lax.slice_in_dim(cells, 0, width, axis=dim)
        tail = lax.slice_in_dim(cells, cells.shape[dim] - width, cells.shape[dim], axis=dim)
        cells = jnp.concatenate(
            [
                lax.ppermute(tail, axis, [(i, (i + 1) % count) for i in range(ends)]),
                cells,
                lax.ppermute(head, axis, [((i + 1) % count, i) for i in range(ends)]),
            ],
            axis=dim,
        )
    return cells


def passed_along(array, axis, by):
    peers = lax.axis_size(axis)
    pairs = [(i, i + by) for i in range(peers) if 0 <= i + by < peers]
    return lax.ppermute(array, axis, pairs)


def shortened(array):
    return jax.tree.map(lambda a: a.astype(jnp.bfloat16) if a.dtype == jnp.float32 else a, array)


def normalize(rows, gain):
    values = rows.astype(jnp.float32)
    scale = lax.rsqrt(jnp.mean(values * values, axis=-1, keepdims=True) + epsilon)
    return ((values * scale * gain).astype(jnp.bfloat16), scale)


def norm_back(rows, scale, gain, grad_norm):
    values = rows.astype(jnp.float32)
    scaled = gain * grad_norm
    return scale * scaled - values * scale**3 * jnp.mean(values * scaled, axis=-1, keepdims=True)


def project(rows, weight):
    return jnp.dot(rows, weight, preferred_element_type=jnp.float32).astype(jnp.bfloat16)


def back_project(rows, weight):
    return lax.dot_general(
        rows, weight, (((1,), (1,)), ((), ())), preferred_element_type=jnp.float32
    )


def exact_back(rows, weight):
    return lax.dot_general(
        rows, weight.astype(jnp.float32), (((1,), (1,)), ((), ())), precision=lax.Precision.HIGHEST
    )


def contract_rows(left, right):
    return lax.dot_general(
        left, right, (((0,), (0,)), ((), ())), preferred_element_type=jnp.float32
    )


def exact_rows(left, right):
    return lax.dot_general(
        left.astype(jnp.float32), right, (((0,), (0,)), ((), ())), precision=lax.Precision.HIGHEST
    )


def grouped(rows, group_width):
    return rows.reshape(rows.shape[0], -1, group_width).transpose(1, 0, 2)


def ungrouped(stacked):
    return stacked.transpose(1, 0, 2).reshape(stacked.shape[1], -1)


def head_scores(query_part, key_part, head_size, factor, allowed):
    query_heads = query_part.reshape(query_part.shape[0], -1, head_size)
    key_heads = key_part.reshape(key_part.shape[0], -1, head_size)
    scores = (
        jnp.einsum("qhd,khd->hqk", query_heads, key_heads, preferred_element_type=jnp.float32)
        * factor
    )
    return jnp.where(allowed[None, None, :], scores, -jnp.inf)


def softmax_grads(
    query_part, key_part, value_part, grad_part, log_totals, row_delta, allowed, head_size, factor
):
    scores = head_scores(query_part, key_part, head_size, factor, allowed)
    weights_full = jnp.exp(scores - log_totals[:, :, None])
    grad_heads = grad_part.reshape(grad_part.shape[0], -1, head_size)
    value_heads = value_part.reshape(value_part.shape[0], -1, head_size)
    grad_weights = jnp.einsum(
        "qhd,khd->hqk", grad_heads, value_heads, preferred_element_type=jnp.float32
    )
    row_delta = jnp.sum(weights_full * grad_weights, axis=-1)
    grad_scores = (weights_full * (grad_weights - row_delta[:, :, None])).astype(jnp.bfloat16)
    return (weights_full.astype(jnp.bfloat16), grad_scores, row_delta)


def key_side(grad_scores, weights_half, query_part, grad_part, head_size, factor):
    query_heads = query_part.reshape(query_part.shape[0], -1, head_size)
    grad_heads = grad_part.reshape(grad_part.shape[0], -1, head_size)
    key_grad = (
        jnp.einsum("hqk,qhd->khd", grad_scores, query_heads, preferred_element_type=jnp.float32)
        * factor
    )
    value_grad = jnp.einsum(
        "hqk,qhd->khd", weights_half, grad_heads, preferred_element_type=jnp.float32
    )
    return (key_grad.reshape(key_grad.shape[0], -1), value_grad.reshape(value_grad.shape[0], -1))


def local(
    tokens, summary, counts, tile_pattern, summary_pattern, norm_gain, projections, cotangent
):
    tile_rows = tokens.shape[2]
    model_width = tokens.shape[3]
    head_size = model_width // HEADS
    group_width = 2 * head_size
    factor = 1.0 / math.sqrt(head_size)
    near_rows = 9 * tile_rows
    zero = jnp.zeros((), jnp.int32)
    grid_row = lax.axis_index("ty")
    grid_col = lax.axis_index("tx")
    token_rows = tokens[0, 0]
    grads_in = cotangent[0, 0]
    w_query, w_key, w_value, w_out = (
        projections[0],
        projections[1],
        projections[2],
        projections[3],
    )
    hidden, row_scale = normalize(token_rows, norm_gain)
    summary_hidden, summary_scale = normalize(summary, norm_gain)
    queries = project(hidden, w_query)
    keys = project(hidden, w_key)
    values = project(hidden, w_value)
    piece = lax.all_gather(summary_hidden, ("ty", "tx"), axis=0, tiled=True)
    every_summary = jnp.concatenate([project(piece, w_key), project(piece, w_value)], axis=1)
    own_pair = jnp.concatenate([keys, values], axis=1).reshape(1, 1, tile_rows, 2 * model_width)
    near_pairs = with_halo(own_pair, (("ty", 0), ("tx", 1)), 1).reshape(near_rows, 2 * model_width)
    all_keys = jnp.concatenate(
        [near_pairs[:, :model_width], every_summary[:, :model_width]], axis=0
    )
    all_values = jnp.concatenate(
        [near_pairs[:, model_width:], every_summary[:, model_width:]], axis=0
    )
    count_pad = jnp.pad(counts, 1)
    near_counts = lax.dynamic_slice(count_pad, (grid_row, grid_col), (3, 3)).reshape(9)
    tile_flags = lax.dynamic_slice(tile_pattern, (grid_row, grid_col, zero), (1, 1, 9)).reshape(9)
    positions = jnp.arange(tile_rows, dtype=jnp.int32)
    tile_ok = ((positions[None, :] < near_counts[:, None]) & (tile_flags[:, None] == 1)).reshape(
        near_rows
    )
    summary_ok = jnp.repeat(summary_pattern[0, 0] == 1, SBLK)
    allowed = jnp.concatenate([tile_ok, summary_ok])
    own_valid = positions < near_counts[4]
    row_mask = own_valid.astype(jnp.float32)[:, None]
    query_groups = grouped(queries, group_width)
    key_groups = grouped(all_keys, group_width)
    value_groups = grouped(all_values, group_width)

    def forward_group(parts):
        query_part, key_part, value_part = parts
        scores = head_scores(query_part, key_part, head_size, factor, allowed)
        largest = jnp.max(scores, axis=-1, keepdims=True)
        exponent = jnp.exp(scores - largest)
        denominator = jnp.sum(exponent, axis=-1, keepdims=True)
        weights_half = (exponent / denominator).astype(jnp.bfloat16)
        value_heads = value_part.reshape(value_part.shape[0], -1, head_size)
        mixed = jnp.einsum(
            "hqk,khd->qhd", weights_half, value_heads, preferred_element_type=jnp.float32
        )
        return (
            mixed.reshape(mixed.shape[0], -1).astype(jnp.bfloat16),
            (largest + jnp.log(denominator))[:, :, 0],
        )

    attended_groups, log_totals = lax.map(forward_group, (query_groups, key_groups, value_groups))
    attended = ungrouped(attended_groups)
    mixed_rows = jnp.dot(attended, w_out, preferred_element_type=jnp.float32)
    updated = (token_rows.astype(jnp.float32) + row_mask * mixed_rows).astype(jnp.bfloat16)
    masked = grads_in * row_mask.astype(jnp.bfloat16)
    attended_grad = back_project(masked, w_out).astype(jnp.bfloat16)
    grad_groups = grouped(attended_grad, group_width)

    def query_group(parts):
        query_part, key_part, value_part, grad_part, log_part = parts
        weights_half, grad_scores, row_delta = softmax_grads(
            query_part, key_part, value_part, grad_part, log_part, None, allowed, head_size, factor
        )
        key_heads = key_part.reshape(key_part.shape[0], -1, head_size)
        query_grad = (
            jnp.einsum("hqk,khd->qhd", grad_scores, key_heads, preferred_element_type=jnp.float32)
            * factor
        )
        summ_kgrad, summ_vgrad = key_side(
            grad_scores[:, :, near_rows:],
            weights_half[:, :, near_rows:],
            query_part,
            grad_part,
            head_size,
            factor,
        )
        outputs = (query_grad.reshape(query_grad.shape[0], -1), summ_kgrad, summ_vgrad, row_delta)
        outputs = outputs + key_side(
            grad_scores[:, :, :near_rows],
            weights_half[:, :, :near_rows],
            query_part,
            grad_part,
            head_size,
            factor,
        )
        return outputs

    results = lax.map(
        query_group, (query_groups, key_groups, value_groups, grad_groups, log_totals)
    )
    query_grad = ungrouped(results[0]).astype(jnp.bfloat16)
    summary_part = jnp.concatenate([ungrouped(results[1]), ungrouped(results[2])], axis=1)
    row_delta = results[3]
    near_grad = jnp.concatenate([ungrouped(results[4]), ungrouped(results[5])], axis=1).reshape(
        3, 3, tile_rows, 2 * model_width
    )
    from_lower = passed_along(near_grad[:, 2].astype(jnp.bfloat16), "tx", 1).astype(jnp.float32)
    from_upper = passed_along(near_grad[:, 0].astype(jnp.bfloat16), "tx", -1).astype(jnp.float32)
    column_sum = near_grad[:, 1] + from_lower + from_upper
    row_lower = passed_along(shortened(column_sum[2]), "ty", 1)
    row_upper = passed_along(shortened(column_sum[0]), "ty", -1)
    own_grad = column_sum[1] + row_lower + row_upper
    key_grad = own_grad[:, :model_width].astype(jnp.bfloat16)
    value_grad = own_grad[:, model_width:].astype(jnp.bfloat16)
    summary_grad = lax.psum_scatter(summary_part, ("ty", "tx"), scatter_dimension=0, tiled=True)
    summary_key_grad = summary_grad[:, :model_width]
    summary_value_grad = summary_grad[:, model_width:]
    summary_hidden_grad = exact_back(summary_key_grad, w_key) + exact_back(
        summary_value_grad, w_value
    )
    summary_key_proj = exact_rows(summary_hidden, summary_key_grad)
    summary_value_proj = exact_rows(summary_hidden, summary_value_grad)
    hidden_grad = (
        back_project(query_grad, w_query)
        + back_project(key_grad, w_key)
        + back_project(value_grad, w_value)
    )
    weight_part = jnp.stack(
        [
            contract_rows(hidden, query_grad),
            contract_rows(hidden, key_grad) + summary_key_proj,
            contract_rows(hidden, value_grad) + summary_value_proj,
            contract_rows(attended, masked),
        ]
    )
    gain_part = jnp.sum(hidden_grad * token_rows.astype(jnp.float32) * row_scale, axis=0) + jnp.sum(
        summary_hidden_grad * summary.astype(jnp.float32) * summary_scale, axis=0
    )
    grad_proj, grad_gain = lax.psum((weight_part, gain_part), ("ty", "tx"))
    grad_tokens = (
        grads_in.astype(jnp.float32) + norm_back(token_rows, row_scale, norm_gain, hidden_grad)
    ).astype(jnp.bfloat16)
    grad_summary = norm_back(summary, summary_scale, norm_gain, summary_hidden_grad).astype(
        jnp.bfloat16
    )
    return (
        updated.reshape(tokens.shape),
        grad_tokens.reshape(tokens.shape),
        grad_summary,
        grad_proj,
        grad_gain,
    )


def solution(mesh):
    return jax.shard_map(
        local,
        mesh=mesh,
        in_specs=(
            P(("slide", "ty"), "tx", None, None),
            P(("slide", "ty", "tx"), None),
            P("slide", None),
            P("slide", None, None),
            P(("slide", "ty"), "tx", None),
            P(),
            P(),
            P(("slide", "ty"), "tx", None, None),
        ),
        out_specs=(
            P(("slide", "ty"), "tx", None, None),
            P(("slide", "ty"), "tx", None, None),
            P(("slide", "ty", "tx"), None),
            P("slide", None, None),
            P("slide"),
        ),
        check_vma=False,
    )
```

profile of v0, /device:TPU:0, one launch (start us, length us, event | category | flops | bytes accessed | tf_op | source)
XLA Modules:
  0.0 711.2 jit_solution(4504195539969881857)
XLA Ops:
  8.4 1.8 convolution_convert_fusion.4
  10.2 1.8 convolution_convert_fusion.5
  12.1 1.4 collective-permute-start.1
  13.6 5.5 collective-permute-start
  20.8 1.7 convolution_convert_fusion.3
  24.6 1.8 convolution_convert_fusion.2
  27.9 3.5 collective-permute-done.1
  33.2 4.7 collective-permute-start.2
  38.2 86.2 %all_gather.3 = bf16[256,768]{1,0:T(8,128)(2,1)S(1)} all-gather(bf16[16,768]{1,0:T(8,128)(2,1)S(1)} %fusion.83), channel_id=1, replica_groups=mesh['ty'=4,'tx'=4,'slide'=2] {'ty','tx'}, dimensions={0}, use_global_device_ids=true | all-gather | bytes 417792 | tf_op jit(solution)/shard_map/all_gather | solution.py:150
  124.4 1.7 convolution_convert_fusion.1
  126.1 1.7 convolution_convert_fusion
  129.0 3.1 pad_maximum_fusion.2
  132.1 3.2 copy.29
  135.2 4.6 copy.30
  139.9 28.4 %while.30 = (s32[]{:T(128)}, bf16[6,192,128]{1,2,0:T(8,128)(2,1)}, f32[6,2,192]{2,1,0:T(2,128)S(1)}, bf16[6,1984,128]{1,2,0:T(8,128)(2,1)S(1)}, pred[1984]{0:T(1...) while((s32[]{:T(128)}, bf16[6,192,128]{1,2,0:T(8,128)(2,1)}, ...), condition=%wide.region_5.6_spmd, body=%wide.region_2.5_spmd.sunk | while | flops 201154176 | bytes 12516909 | solution.py:191
  168.3 59.4 %while.31 = (s32[]{:T(128)}, bf16[6,192,128]{1,2,0:T(8,128)(2,1)}, f32[6,256,128]{1,2,0:T(8,128)}, f32[6,256,128]{1,2,0:T(8,128)}, f32[6,1728,128]{1,2,0:T(8,128...) while((s32[]{:T(128)}, bf16[6,192,128]{1,2,0:T(8,128)(2,1)}, ...), condition=%wide.region_8.9_spmd, body=%wide.region_6.8_spmd.sunk | while | flops 494747264 | bytes 33400420 | solution.py:228
  186.6 1.4 constant_dynamic-update-slice_fusion.15
  196.6 1.4 constant_dynamic-update-slice_fusion.15
  206.4 1.4 constant_dynamic-update-slice_fusion.15
  216.3 1.4 constant_dynamic-update-slice_fusion.15
  226.2 1.4 constant_dynamic-update-slice_fusion.15
  227.6 7.5 %copy.34 = f32[1728,6,128]{2,1,0:T(8,128)} copy(f32[1728,6,128]{0,2,1:T(8,128)} %bitcast.284) | data formatting | bytes 10616832 | tf_op jit(solution)/shard_map/transpose | solution.py:84
  235.1 7.1 concatenate.35
  242.2 5.4 constant_dynamic-update-slice_fusion.7
  247.6 7.5 %copy.35 = f32[1728,6,128]{2,1,0:T(8,128)} copy(f32[1728,6,128]{0,2,1:T(8,128)} %bitcast.285) | data formatting | bytes 10616832 | tf_op jit(solution)/shard_map/transpose | solution.py:84
  255.1 7.1 %concatenate.36 = f32[3,3,192,768]{3,2,1,0:T(8,128)} reshape(f32[1728,6,128]{2,1,0:T(8,128)} %copy.35) | data formatting | bytes 10616832 | tf_op jit(solution)/shard_map/concatenate | solution.py:234
  262.2 5.4 constant_dynamic-update-slice_fusion.6
  267.6 4.7 convert.14
  272.4 2.0 slice_bitcast_fusion.2
  275.7 5.8 collective-permute-start.4
  281.6 1.6 copy.37
  283.5 30.0 %collective-permute-done.5 = bf16[3,192,1536]{2,1,0:T(8,128)(2,1)} collective-permute-done((bf16[3,192,1536]{2,1,0:T(8,128)(2,1)}, bf16[3,192,1536]{2,1,0:T(8,128)(2,1)}, u32[]{:S(2)}, u32[]{:S(2)}) %collective-permute-start.5) | collective-permute-done | bytes 1769504 | tf_op jit(solution)/shard_map/ppermute | solution.py:32
  313.5 2.0 collective-permute-done.4
  315.5 3.9 fusion.102
  319.5 1.4 collective-permute-start.7
  320.9 4.6 collective-permute-start.6
  326.1 2.0 convolution_bitcast_fusion.1
  328.1 4.3 collective-permute-done.7
  333.5 74.2 %reduce-scatter.4.cloned.1.call-done = f32[16,1536]{1,0:T(8,128)} async-done(((f32[256,1536]{1,0:T(8,128)}), f32[16,1536]{1,0:T(8,128)}) %reduce-scatter.4.cloned.1.call-update) | async-done | bytes 98320
  407.6 1.9 fusion.91
  413.2 4.0 pad_maximum_fusion
  418.3 2.6 fusion.32
  420.9 2.1 fusion.19
  423.0 1.9 convolution_add_fusion.1
  424.9 2.0 fusion.64
  430.0 42.8 %psum.15 = f32[768]{0:T(1024)} all-reduce(f32[768]{0:T(1024)S(1)} %add.120), channel_id=1, replica_groups=mesh['ty'=4,'tx'=4,'slide'=2] {'ty','tx'}, use_global_device_ids=true, to_apply=%region_15.16 | all-reduce | flops 768 | bytes 6144 | tf_op jit(solution)/shard_map/psum | solution.py:269
  473.5 222.8 %all-reduce.3.cloned.1.call-done = f32[4,768,768]{2,1,0:T(8,128)} async-done(((f32[4,768,768]{2,1,0:T(8,128)}), f32[4,768,768]{2,1,0:T(8,128)}) %all-reduce.3.cloned.1.call-update) | async-done | bytes 9437200 | tf_op jit(solution)/shard_map/psum | solution.py:269
  696.3 8.0 %copy.80 = f32[4,768,768]{2,1,0:T(8,128)} copy(f32[4,768,768]{2,1,0:T(8,128)} %all-reduce.3.cloned.1.call-done) | data formatting | bytes 18874368
  (225 shorter events, 101.8 us)
Async XLA Ops:
  7.2 13.7 %copy-start.1 = (bf16[1,1,192,768]{3,2,1,0:T(8,128)(2,1)S(1)}, bf16[1,1,192,768]{3,2,1,0:T(8,128)(2,1)}, u32[]{:S(2)}) copy-start(bf16[1,1,192,768]{3,2,1,0:T(8,128)(2,1)} %param.12) | copy-start | bytes 884740
  7.2 13.7 %copy-start.13 = (f32[768]{0:T(1024)S(1)}, f32[768]{0:T(1024)}, u32[]{:S(2)}) copy-start(f32[768]{0:T(1024)} %param.17) | copy-start | bytes 9220
  7.2 12.0 %copy-start.14 = (s32[4,4]{1,0:T(4,128)S(1)}, s32[4,4]{1,0:T(4,128)}, u32[]{:S(2)}) copy-start(s32[4,4]{1,0:T(4,128)} %param.14) | copy-start | bytes 196
  7.2 400.4 %reduce-scatter.4.cloned.1.call-start = ((), (), s32[]{:S(2)}) async-start(), calls=%async_computation.2 | async-start | bytes 1671168
  12.1 12.5 %copy-start.4 = (bf16[1,1,192,768]{3,2,1,0:T(8,128)(2,1)S(1)}, bf16[1,1,192,768]{3,2,1,0:T(8,128)(2,1)}, u32[]{:S(2)}) copy-start(bf16[1,1,192,768]{3,2,1,0:T(8,128)(2,1)} %param.19) | copy-start | bytes 884740
  12.1 19.2 %collective-permute-start.1 = (bf16[1,1,192,1536]{3,2,1,0:T(8,128)(2,1)S(1)}, bf16[1,1,192,1536]{3,2,1,0:T(8,128)(2,1)S(1)}, u32[]{:S(2)}, u32[]{:S(2)}) collective-permute-start(bf16[1,1,192,1536]{3,2,1,0:T(8,128)(2,1)S(1)} %maximum_bitcast_fusion), channel_id=1, source_target_pairs={{8,0},{16,8},{24,16},{9,1},{17,9},{25,17},{10,2},{18,10},{26,18},{... | collective-permute-start | bytes 1769480 | tf_op jit(solution)/shard_map/ppermute | solution.py:22
  13.6 18.1 %collective-permute-start = (bf16[1,1,192,1536]{3,2,1,0:T(8,128)(2,1)S(1)}, bf16[1,1,192,1536]{3,2,1,0:T(8,128)(2,1)S(1)}, u32[]{:S(2)}, u32[]{:S(2)}) collective-permute-start(bf16[1,1,192,1536]{3,2,1,0:T(8,128)(2,1)S(1)} %maximum_bitcast_fusion), channel_id=1, source_target_pairs={{0,8},{8,16},{16,24},{1,9},{9,17},{17,25},{2,10},{10,18},{18,26},{... | collective-permute-start | bytes 1769480 | tf_op jit(solution)/shard_map/ppermute | solution.py:20
  24.6 13.2 %copy-start.15 = (s32[1,1,2]{2,1,0:T(1,128)S(1)}, s32[1,1,2]{2,1,0:T(1,128)}, u32[]{:S(2)}) copy-start(s32[1,1,2]{2,1,0:T(1,128)} %param.16) | copy-start | bytes 28
  24.6 13.4 %copy-start.12 = (bf16[16,768]{1,0:T(8,128)(2,1)S(1)}, bf16[16,768]{1,0:T(8,128)(2,1)}, u32[]{:S(2)}) copy-start(bf16[16,768]{1,0:T(8,128)(2,1)} %param.13) | copy-start | bytes 73732
  31.9 96.1 %collective-permute-start.3 = (bf16[3,1,192,1536]{3,2,1,0:T(8,128)(2,1)S(1)}, bf16[3,1,192,1536]{3,2,1,0:T(8,128)(2,1)S(1)}, u32[]{:S(2)}, u32[]{:S(2)}) collective-permute-start(bf16[3,1,192,1536]{3,2,1,0:T(8,128)(2,1)S(1)} %pad_maximum_fusion.4), channel_id=1, source_target_pairs={{2,0},{4,2},{6,4},{3,1},{5,3},{7,5},{10,8},{12,10},{14,12},{11,9},... | collective-permute-start | bytes 5308424 | tf_op jit(solution)/shard_map/ppermute | solution.py:22
  33.2 94.8 %collective-permute-start.2 = (bf16[3,1,192,1536]{3,2,1,0:T(8,128)(2,1)S(1)}, bf16[3,1,192,1536]{3,2,1,0:T(8,128)(2,1)S(1)}, u32[]{:S(2)}, u32[]{:S(2)}) collective-permute-start(bf16[3,1,192,1536]{3,2,1,0:T(8,128)(2,1)S(1)} %pad_maximum_fusion.4), channel_id=1, source_target_pairs={{0,2},{2,4},{4,6},{1,3},{3,5},{5,7},{8,10},{10,12},{12,14},{9,11},... | collective-permute-start | bytes 5308424 | tf_op jit(solution)/shard_map/ppermute | solution.py:20
  272.4 9.2 %copy-start.7 = (f32[6,256,128]{1,2,0:T(8,128)S(1)}, f32[6,256,128]{1,2,0:T(8,128)}, u32[]{:S(2)}) copy-start(f32[6,256,128]{1,2,0:T(8,128)} %get-tuple-element.114) | copy-start | bytes 2359300
  272.4 9.1 %copy-start.8 = (f32[6,256,128]{1,2,0:T(8,128)S(1)}, f32[6,256,128]{1,2,0:T(8,128)}, u32[]{:S(2)}) copy-start(f32[6,256,128]{1,2,0:T(8,128)} %get-tuple-element.115) | copy-start | bytes 2359300
  274.4 39.1 %collective-permute-start.5 = (bf16[3,192,1536]{2,1,0:T(8,128)(2,1)}, bf16[3,192,1536]{2,1,0:T(8,128)(2,1)}, u32[]{:S(2)}, u32[]{:S(2)}) collective-permute-start(bf16[3,192,1536]{2,1,0:T(8,128)(2,1)} %get-tuple-element.211), channel_id=1, source_target_pairs={{2,0},{4,2},{6,4},{3,1},{5,3},{7,5},{10,8},{12,10},{14,12},{11,9},... | collective-permute-start | bytes 5308424 | tf_op jit(solution)/shard_map/ppermute | solution.py:32
  275.7 39.8 %collective-permute-start.4 = (bf16[3,192,1536]{2,1,0:T(8,128)(2,1)}, bf16[3,192,1536]{2,1,0:T(8,128)(2,1)}, u32[]{:S(2)}, u32[]{:S(2)}) collective-permute-start(bf16[3,192,1536]{2,1,0:T(8,128)(2,1)} %get-tuple-element.210), channel_id=1, source_target_pairs={{0,2},{2,4},{4,6},{1,3},{3,5},{5,7},{8,10},{10,12},{12,14},{9,11},... | collective-permute-start | bytes 5308424 | tf_op jit(solution)/shard_map/ppermute | solution.py:32
  283.2 42.3 %copy-start.5 = (bf16[1,1,192,768]{3,2,1,0:T(8,128)(2,1)S(1)}, bf16[1,1,192,768]{3,2,1,0:T(8,128)(2,1)}, u32[]{:S(2)}) copy-start(bf16[1,1,192,768]{3,2,1,0:T(8,128)(2,1)} %param.19) | copy-start | bytes 884740
  283.3 413.1 %all-reduce.3.cloned.1.call-start = ((), (), s32[]{:S(2)}) async-start(), calls=%async_computation.1 | async-start | bytes 18874368 | tf_op jit(solution)/shard_map/psum | solution.py:269
  283.5 42.0 %copy-start.9 = (bf16[6,192,128]{1,2,0:T(8,128)(2,1)S(1)}, bf16[6,192,128]{1,2,0:T(8,128)(2,1)}, u32[]{:S(2)}) copy-start(bf16[6,192,128]{1,2,0:T(8,128)(2,1)} %get-tuple-element.109) | copy-start | bytes 884740
  319.4 6.7 copy-start.2
  319.5 12.9 %collective-permute-start.7 = (bf16[192,1536]{1,0:T(8,128)(2,1)S(1)}, bf16[192,1536]{1,0:T(8,128)(2,1)S(1)}, u32[]{:S(2)}, u32[]{:S(2)}) collective-permute-start(bf16[192,1536]{1,0:T(8,128)(2,1)S(1)} %get-tuple-element.215), channel_id=1, source_target_pairs={{8,0},{16,8},{24,16},{9,1},{17,9},{25,17},{10,2},{18,10},{26,18},{... | collective-permute-start | bytes 1769480 | tf_op jit(solution)/shard_map/ppermute | solution.py:32
  320.9 12.3 %collective-permute-start.6 = (bf16[192,1536]{1,0:T(8,128)(2,1)S(1)}, bf16[192,1536]{1,0:T(8,128)(2,1)S(1)}, u32[]{:S(2)}, u32[]{:S(2)}) collective-permute-start(bf16[192,1536]{1,0:T(8,128)(2,1)S(1)} %get-tuple-element.214), channel_id=1, source_target_pairs={{0,8},{8,16},{16,24},{1,9},{9,17},{17,25},{2,10},{10,18},{18,26},{... | collective-permute-start | bytes 1769480 | tf_op jit(solution)/shard_map/ppermute | solution.py:32
  409.6 0.9 copy-start.11
  411.6 1.7 copy-start
  417.3 1.0 copy-start.10
  417.3 3.6 copy-start.3
  417.3 10.5 %slice-start = ((s8[4718592]{0:T(1024)(128)(4,1)}), s8[524288]{0:T(1024)(128)(4,1)S(1)}, s32[]{:S(2)}) async-start(s8[4718592]{0:T(1024)(128)(4,1)} %bitcast.286), calls=%async_computation.3 | async-start | bytes 1048576
  418.3 9.5 %slice-start.1 = ((s8[4718592]{0:T(1024)(128)(4,1)}), s8[4194304]{0:T(1024)(128)(4,1)S(1)}, s32[]{:S(2)}) async-start(s8[4718592]{0:T(1024)(128)(4,1)} %bitcast.286), calls=%async_computation.4 | async-start | bytes 8388608
  422.9 3.9 copy-start.6
Sparse Core Ops, SparseCore 0:
  283.4 124.2 reduce-scatter.3
  417.4 278.8 all-reduce.2
where the time goes:
time: 714 us; the launch traced here: 711 us
  waiting for transfers between devices  338 us (47%)
  blocking collectives  129 us (18%)
  local copies, waits for them, and re-layouts  114 us (16%)
  matrix products  59.7 us (8%)
  other arithmetic  29.2 us (4%)
  starting transfers between devices  26.3 us (4%)
  between operations  14.6 us (2%)
    psum x1, waiting for transfers between devices, local(): grad_proj, grad_gain = lax.psum((weight_part, gain_part), ('ty', 'tx'))  223 us
    all_gather x1, blocking collectives, local(): piece = lax.all_gather(summary_hidden, ('ty', 'tx'), axis=0, tiled=True)  86.2 us
    unnamed x3, waiting for transfers between devices  74.2 us
    psum x1, blocking collectives, local(): grad_proj, grad_gain = lax.psum((weight_part, gain_part), ('ty', 'tx'))  42.8 us
    ppermute x4, waiting for transfers between devices, passed_along(): return lax.ppermute(array, axis, pairs)  37.1 us
    dynamic_slice x36, local copies, waits for them, and re-layouts, local(): lax.map(forward_group, (query_groups, key_groups, value_groups))  28.7 us
    concatenate x3, local copies, waits for them, and re-layouts, local(): jnp.concatenate([ungrouped(results[4]), ungrouped(results[5])], axis=1)  19.6 us
    unnamed x39, local copies, waits for them, and re-layouts  16.6 us
  transfers between devices with their start and end apart: 10, of which 8 were waited for; matrix products, arithmetic and copies ran while one was open for 5% of the time, Pallas kernels for 0%

commit v1 on v0

--- a/solution.py
+++ b/solution.py
@@ -266,7 +266,13 @@
     gain_part = jnp.sum(hidden_grad * token_rows.astype(jnp.float32) * row_scale, axis=0) + jnp.sum(
         summary_hidden_grad * summary.astype(jnp.float32) * summary_scale, axis=0
     )
-    grad_proj, grad_gain = lax.psum((weight_part, gain_part), ("ty", "tx"))
+
+    def _point_copies(sample):
+        for hop_no in ("tx", "ty"):
+            sample = lax.psum(sample, axis_name=hop_no)
+        return sample
+
+    grad_proj, grad_gain = _point_copies((weight_part, gain_part))
     grad_tokens = (
         grads_in.astype(jnp.float32) + norm_back(token_rows, row_scale, norm_gain, hidden_grad)
     ).astype(jnp.bfloat16)

time: 714 us -> 951 us (1.33)
  waiting for transfers between devices: 338 us -> 596 us
  blocking collectives: 129 us -> 106 us
    psum x1 -> x2, waiting for transfers between devices: 223 us -> 481 us  [_point_copies(): sample = lax.psum(sample, axis_name=hop_no)]
    psum x1 -> x2, blocking collectives: 42.8 us -> 20.2 us  [_point_copies(): sample = lax.psum(sample, axis_name=hop_no)]
    unnamed x3 -> x4, waiting for transfers between devices: 74.2 us -> 74.3 us
  transfers between devices with their start and end apart: 10 -> 11, of which waited for: 8 -> 9; matrix products, arithmetic and copies ran while one was open for 5% -> 4% of each run, Pallas kernels for 0% -> 0%
where the time goes in v1:
time: 951 us; the launch traced here: 948 us
  waiting for transfers between devices  596 us (63%)
  local copies, waits for them, and re-layouts  114 us (12%)
  blocking collectives  106 us (11%)
  matrix products  59.8 us (6%)
  other arithmetic  29.7 us (3%)
  starting transfers between devices  26.3 us (3%)
  between operations  14.3 us (2%)
    psum x2, waiting for transfers between devices, _point_copies(): sample = lax.psum(sample, axis_name=hop_no)  481 us
    all_gather x1, blocking collectives, local(): piece = lax.all_gather(summary_hidden, ('ty', 'tx'), axis=0, tiled=True)  86.2 us
    unnamed x4, waiting for transfers between devices  74.3 us
    ppermute x4, waiting for transfers between devices, passed_along(): return lax.ppermute(array, axis, pairs)  37.1 us
    dynamic_slice x36, local copies, waits for them, and re-layouts, local(): lax.map(forward_group, (query_groups, key_groups, value_groups))  28.7 us
    psum x2, blocking collectives, _point_copies(): sample = lax.psum(sample, axis_name=hop_no)  20.2 us
    concatenate x3, local copies, waits for them, and re-layouts, local(): jnp.concatenate([ungrouped(results[4]), ungrouped(results[5])], axis=1)  19.7 us
  transfers between devices with their start and end apart: 11, of which 9 were waited for; matrix products, arithmetic and copies ran while one was open for 4% of the time, Pallas kernels for 0%

profile of v1, /device:TPU:0, one launch (start us, length us, event | category | flops | bytes accessed | tf_op | source)
XLA Modules:
  0.0 947.5 jit_solution(2658482670735750148)
XLA Ops:
  9.0 1.8 convolution_convert_fusion.4
  10.8 1.8 convolution_convert_fusion.5
  12.7 1.4 collective-permute-start.1
  14.1 5.5 collective-permute-start
  21.4 1.7 convolution_convert_fusion.3
  25.2 1.8 convolution_convert_fusion.2
  28.4 3.5 collective-permute-done.1
  33.7 4.7 collective-permute-start.2
  38.8 86.2 %all_gather.3 = bf16[256,768]{1,0:T(8,128)(2,1)S(1)} all-gather(bf16[16,768]{1,0:T(8,128)(2,1)S(1)} %fusion.83), channel_id=1, replica_groups=mesh['ty'=4,'tx'=4,'slide'=2] {'ty','tx'}, dimensions={0}, use_global_device_ids=true | all-gather | bytes 417792 | tf_op jit(solution)/shard_map/all_gather | solution.py:150
  125.0 1.7 convolution_convert_fusion.1
  126.7 1.7 convolution_convert_fusion
  129.5 3.0 pad_maximum_fusion.2
  132.6 3.2 copy.29
  135.7 4.6 copy.30
  140.4 28.4 %while.30 = (s32[]{:T(128)}, bf16[6,192,128]{1,2,0:T(8,128)(2,1)}, f32[6,2,192]{2,1,0:T(2,128)S(1)}, bf16[6,1984,128]{1,2,0:T(8,128)(2,1)S(1)}, pred[1984]{0:T(1...) while((s32[]{:T(128)}, bf16[6,192,128]{1,2,0:T(8,128)(2,1)}, ...), condition=%wide.region_5.6_spmd, body=%wide.region_2.5_spmd.sunk | while | flops 201154176 | bytes 12516909 | solution.py:191
  168.8 59.4 %while.31 = (s32[]{:T(128)}, bf16[6,192,128]{1,2,0:T(8,128)(2,1)}, f32[6,256,128]{1,2,0:T(8,128)}, f32[6,256,128]{1,2,0:T(8,128)}, f32[6,1728,128]{1,2,0:T(8,128...) while((s32[]{:T(128)}, bf16[6,192,128]{1,2,0:T(8,128)(2,1)}, ...), condition=%wide.region_8.9_spmd, body=%wide.region_6.8_spmd.sunk | while | flops 494747264 | bytes 33400420 | solution.py:228
  187.2 1.4 constant_dynamic-update-slice_fusion.15
  216.8 1.4 constant_dynamic-update-slice_fusion.15
  226.7 1.4 constant_dynamic-update-slice_fusion.15
  228.2 7.5 copy.34
  235.7 7.1 concatenate.35
  242.8 5.4 constant_dynamic-update-slice_fusion.7
  248.1 7.5 copy.35
  255.7 7.1 concatenate.36
  262.8 5.5 constant_dynamic-update-slice_fusion.6
  268.2 4.7 convert.14
  273.0 2.0 slice_bitcast_fusion.2
  276.3 5.8 collective-permute-start.4
  282.2 1.6 copy.37
  284.1 30.0 %collective-permute-done.5 = bf16[3,192,1536]{2,1,0:T(8,128)(2,1)} collective-permute-done((bf16[3,192,1536]{2,1,0:T(8,128)(2,1)}, bf16[3,192,1536]{2,1,0:T(8,128)(2,1)}, u32[]{:S(2)}, u32[]{:S(2)}) %collective-permute-start.5) | collective-permute-done | bytes 1769504 | tf_op jit(solution)/shard_map/ppermute | solution.py:32
  314.1 2.0 collective-permute-done.4
  316.1 3.9 fusion.102
  320.1 1.4 collective-permute-start.7
  321.5 4.6 collective-permute-start.6
  326.7 2.0 convolution_bitcast_fusion.1
  328.7 4.3 collective-permute-done.7
  334.1 74.2 %reduce-scatter.4.cloned.1.call-done = f32[16,1536]{1,0:T(8,128)} async-done(((f32[256,1536]{1,0:T(8,128)}), f32[16,1536]{1,0:T(8,128)}) %reduce-scatter.4.cloned.1.call-update) | async-done | bytes 98320
  408.3 1.9 fusion.91
  413.9 4.0 pad_maximum_fusion
  418.0 323.7 %all-reduce.4.cloned.1.call-done = f32[4,768,768]{2,1,0:T(8,128)} async-done(((f32[4,768,768]{2,1,0:T(8,128)}), f32[4,768,768]{2,1,0:T(8,128)}) %all-reduce.4.cloned.1.call-update) | async-done | bytes 9437200 | tf_op jit(solution)/shard_map/psum | solution.py:272
  742.8 2.6 fusion.32
  745.3 1.8 fusion.19
  747.2 1.9 convolution_add_fusion.1
  749.0 2.3 fusion.64
  754.6 9.1 psum.30
  763.7 11.1 %psum.31 = f32[768]{0:T(1024)} all-reduce(f32[768]{0:T(1024)S(1)} %psum.30), channel_id=1, replica_groups=mesh['ty'=4,'tx'=4,'slide'=2] {'ty'}, use_global_device_ids=true, to_apply=%region_17.18 | all-reduce | flops 768 | bytes 6144 | tf_op jit(solution)/shard_map/psum | solution.py:272
  775.5 157.5 %all-reduce.6.cloned.1.call-done = f32[4,768,768]{2,1,0:T(8,128)} async-done(((f32[4,768,768]{2,1,0:T(8,128)}), f32[4,768,768]{2,1,0:T(8,128)}) %all-reduce.6.cloned.1.call-update) | async-done | bytes 9437200 | tf_op jit(solution)/shard_map/psum | solution.py:272
  933.0 8.0 copy.81
  (231 shorter events, 105.2 us)
Async XLA Ops:
  7.2 14.2 %copy-start.1 = (bf16[1,1,192,768]{3,2,1,0:T(8,128)(2,1)S(1)}, bf16[1,1,192,768]{3,2,1,0:T(8,128)(2,1)}, u32[]{:S(2)}) copy-start(bf16[1,1,192,768]{3,2,1,0:T(8,128)(2,1)} %param.12) | copy-start | bytes 884740
  7.2 14.2 %copy-start.13 = (f32[768]{0:T(1024)S(1)}, f32[768]{0:T(1024)}, u32[]{:S(2)}) copy-start(f32[768]{0:T(1024)} %param.17) | copy-start | bytes 9220
  7.2 12.6 %copy-start.15 = (s32[4,4]{1,0:T(4,128)S(1)}, s32[4,4]{1,0:T(4,128)}, u32[]{:S(2)}) copy-start(s32[4,4]{1,0:T(4,128)} %param.14) | copy-start | bytes 196
  7.2 401.1 %reduce-scatter.4.cloned.1.call-start = ((), (), s32[]{:S(2)}) async-start(), calls=%async_computation.3 | async-start | bytes 1671168
  12.6 12.5 %copy-start.4 = (bf16[1,1,192,768]{3,2,1,0:T(8,128)(2,1)S(1)}, bf16[1,1,192,768]{3,2,1,0:T(8,128)(2,1)}, u32[]{:S(2)}) copy-start(bf16[1,1,192,768]{3,2,1,0:T(8,128)(2,1)} %param.19) | copy-start | bytes 884740
  12.7 19.2 %collective-permute-start.1 = (bf16[1,1,192,1536]{3,2,1,0:T(8,128)(2,1)S(1)}, bf16[1,1,192,1536]{3,2,1,0:T(8,128)(2,1)S(1)}, u32[]{:S(2)}, u32[]{:S(2)}) collective-permute-start(bf16[1,1,192,1536]{3,2,1,0:T(8,128)(2,1)S(1)} %maximum_bitcast_fusion), channel_id=1, source_target_pairs={{8,0},{16,8},{24,16},{9,1},{17,9},{25,17},{10,2},{18,10},{26,18},{... | collective-permute-start | bytes 1769480 | tf_op jit(solution)/shard_map/ppermute | solution.py:22
  14.1 18.1 %collective-permute-start = (bf16[1,1,192,1536]{3,2,1,0:T(8,128)(2,1)S(1)}, bf16[1,1,192,1536]{3,2,1,0:T(8,128)(2,1)S(1)}, u32[]{:S(2)}, u32[]{:S(2)}) collective-permute-start(bf16[1,1,192,1536]{3,2,1,0:T(8,128)(2,1)S(1)} %maximum_bitcast_fusion), channel_id=1, source_target_pairs={{0,8},{8,16},{16,24},{1,9},{9,17},{17,25},{2,10},{10,18},{18,26},{... | collective-permute-start | bytes 1769480 | tf_op jit(solution)/shard_map/ppermute | solution.py:20
  25.2 13.2 %copy-start.16 = (s32[1,1,2]{2,1,0:T(1,128)S(1)}, s32[1,1,2]{2,1,0:T(1,128)}, u32[]{:S(2)}) copy-start(s32[1,1,2]{2,1,0:T(1,128)} %param.16) | copy-start | bytes 28
  25.2 13.4 %copy-start.12 = (bf16[16,768]{1,0:T(8,128)(2,1)S(1)}, bf16[16,768]{1,0:T(8,128)(2,1)}, u32[]{:S(2)}) copy-start(bf16[16,768]{1,0:T(8,128)(2,1)} %param.13) | copy-start | bytes 73732
  32.4 96.1 %collective-permute-start.3 = (bf16[3,1,192,1536]{3,2,1,0:T(8,128)(2,1)S(1)}, bf16[3,1,192,1536]{3,2,1,0:T(8,128)(2,1)S(1)}, u32[]{:S(2)}, u32[]{:S(2)}) collective-permute-start(bf16[3,1,192,1536]{3,2,1,0:T(8,128)(2,1)S(1)} %pad_maximum_fusion.4), channel_id=1, source_target_pairs={{2,0},{4,2},{6,4},{3,1},{5,3},{7,5},{10,8},{12,10},{14,12},{11,9},... | collective-permute-start | bytes 5308424 | tf_op jit(solution)/shard_map/ppermute | solution.py:22
  33.7 94.8 %collective-permute-start.2 = (bf16[3,1,192,1536]{3,2,1,0:T(8,128)(2,1)S(1)}, bf16[3,1,192,1536]{3,2,1,0:T(8,128)(2,1)S(1)}, u32[]{:S(2)}, u32[]{:S(2)}) collective-permute-start(bf16[3,1,192,1536]{3,2,1,0:T(8,128)(2,1)S(1)} %pad_maximum_fusion.4), channel_id=1, source_target_pairs={{0,2},{2,4},{4,6},{1,3},{3,5},{5,7},{8,10},{10,12},{12,14},{9,11},... | collective-permute-start | bytes 5308424 | tf_op jit(solution)/shard_map/ppermute | solution.py:20
  273.0 9.1 copy-start.7
  273.0 9.1 copy-start.8
  275.0 39.1 %collective-permute-start.5 = (bf16[3,192,1536]{2,1,0:T(8,128)(2,1)}, bf16[3,192,1536]{2,1,0:T(8,128)(2,1)}, u32[]{:S(2)}, u32[]{:S(2)}) collective-permute-start(bf16[3,192,1536]{2,1,0:T(8,128)(2,1)} %get-tuple-element.211), channel_id=1, source_target_pairs={{2,0},{4,2},{6,4},{3,1},{5,3},{7,5},{10,8},{12,10},{14,12},{11,9},... | collective-permute-start | bytes 5308424 | tf_op jit(solution)/shard_map/ppermute | solution.py:32
  276.3 39.8 %collective-permute-start.4 = (bf16[3,192,1536]{2,1,0:T(8,128)(2,1)}, bf16[3,192,1536]{2,1,0:T(8,128)(2,1)}, u32[]{:S(2)}, u32[]{:S(2)}) collective-permute-start(bf16[3,192,1536]{2,1,0:T(8,128)(2,1)} %get-tuple-element.210), channel_id=1, source_target_pairs={{0,2},{2,4},{4,6},{1,3},{3,5},{5,7},{8,10},{10,12},{12,14},{9,11},... | collective-permute-start | bytes 5308424 | tf_op jit(solution)/shard_map/ppermute | solution.py:32
  283.8 42.3 %copy-start.5 = (bf16[1,1,192,768]{3,2,1,0:T(8,128)(2,1)S(1)}, bf16[1,1,192,768]{3,2,1,0:T(8,128)(2,1)}, u32[]{:S(2)}) copy-start(bf16[1,1,192,768]{3,2,1,0:T(8,128)(2,1)} %param.19) | copy-start | bytes 884740
  283.9 457.9 %all-reduce.4.cloned.1.call-start = ((), (), s32[]{:S(2)}) async-start(), calls=%async_computation.1 | async-start | bytes 18874368 | tf_op jit(solution)/shard_map/psum | solution.py:272
  284.1 42.0 %copy-start.9 = (bf16[6,192,128]{1,2,0:T(8,128)(2,1)S(1)}, bf16[6,192,128]{1,2,0:T(8,128)(2,1)}, u32[]{:S(2)}) copy-start(bf16[6,192,128]{1,2,0:T(8,128)(2,1)} %get-tuple-element.109) | copy-start | bytes 884740
  320.0 6.7 copy-start.2
  320.1 12.9 %collective-permute-start.7 = (bf16[192,1536]{1,0:T(8,128)(2,1)S(1)}, bf16[192,1536]{1,0:T(8,128)(2,1)S(1)}, u32[]{:S(2)}, u32[]{:S(2)}) collective-permute-start(bf16[192,1536]{1,0:T(8,128)(2,1)S(1)} %get-tuple-element.215), channel_id=1, source_target_pairs={{8,0},{16,8},{24,16},{9,1},{17,9},{25,17},{10,2},{18,10},{26,18},{... | collective-permute-start | bytes 1769480 | tf_op jit(solution)/shard_map/ppermute | solution.py:32
  321.5 12.3 %collective-permute-start.6 = (bf16[192,1536]{1,0:T(8,128)(2,1)S(1)}, bf16[192,1536]{1,0:T(8,128)(2,1)S(1)}, u32[]{:S(2)}, u32[]{:S(2)}) collective-permute-start(bf16[192,1536]{1,0:T(8,128)(2,1)S(1)} %get-tuple-element.214), channel_id=1, source_target_pairs={{0,8},{8,16},{16,24},{1,9},{9,17},{17,25},{2,10},{10,18},{18,26},{... | collective-permute-start | bytes 1769480 | tf_op jit(solution)/shard_map/ppermute | solution.py:32
  410.2 0.9 copy-start.11
  412.3 1.7 copy-start
  418.0 515.0 %all-reduce.6.cloned.1.call-start = ((), (), s32[]{:S(2)}) async-start(), calls=%async_computation.2 | async-start | bytes 18874368 | tf_op jit(solution)/shard_map/psum | solution.py:272
  741.8 1.0 copy-start.10
  741.8 3.6 copy-start.3
  741.8 10.6 %slice-start = ((s8[4718592]{0:T(1024)(128)(4,1)}), s8[524288]{0:T(1024)(128)(4,1)S(1)}, s32[]{:S(2)}) async-start(s8[4718592]{0:T(1024)(128)(4,1)} %bitcast.286), calls=%async_computation.4 | async-start | bytes 1048576
  742.8 9.6 %slice-start.1 = ((s8[4718592]{0:T(1024)(128)(4,1)}), s8[4194304]{0:T(1024)(128)(4,1)S(1)}, s32[]{:S(2)}) async-start(s8[4718592]{0:T(1024)(128)(4,1)} %bitcast.286), calls=%async_computation.5 | async-start | bytes 8388608
  747.2 4.2 copy-start.6
  747.2 4.2 copy-start.14
Sparse Core Ops, SparseCore 0:
  284.0 124.2 reduce-scatter.3
  418.1 323.6 all-reduce.3
  745.3 187.6 all-reduce.5
